TPU v7x, 32 devices: a whole 2x2x4 slice. The times are simulated.
32 devices in a mesh: groups: 2 (over x), lon: 16 (over z, y, core).
Axes of the slice: x: 2, y: 2, z: 4, core: 2. Of those that a mesh axis runs over, the one named last changes fastest.
Arguments:
- fields: bfloat16 [32, 32, 1500], P(('groups', 'lon')), parts along dimension 0, may hold values from -6 to 6
- level_ids: int32 [6], P('groups'), parts along dimension 0, may hold values from 0 to 2, each once
- embed_weight: bfloat16 [500, 512], replicated, may hold values from -0.25 to 0.25
- level_embed: bfloat16 [3, 512], replicated, may hold values from -6 to 6
- enc_gain: float32 [512], replicated, may hold values from 0.1 to 1.9
- latent_query: bfloat16 [2, 512], replicated, may hold values from -0.049804688 to 0.049804688
- kv_weight: bfloat16 [512, 1024], replicated, may hold values from -0.25 to 0.25
- pool_out: bfloat16 [512, 512], replicated, may hold values from -0.25 to 0.25
- attn_gain: float32 [512], replicated, may hold values from 0.1 to 1.9
- qkv_weight: bfloat16 [512, 1536], replicated, may hold values from -0.25 to 0.25
- attn_proj: bfloat16 [512, 512], replicated, may hold values from -0.25 to 0.25
- mlp_gain: float32 [512], replicated, may hold values from 0.1 to 1.9
- mlp_up: bfloat16 [512, 2048], replicated, may hold values from -0.25 to 0.25
- mlp_down: bfloat16 [2048, 512], replicated, may hold values from -0.125 to 0.125
- level_mix: float32 [3, 2], replicated, may hold values from 0.25 to 4
- dec_gain: float32 [512], replicated, may hold values from 0.1 to 1.9
- dec_weight: bfloat16 [512, 500], replicated, may hold values from -0.25 to 0.25
Outputs:
- forecast: bfloat16 [32, 32, 1500], P(('groups', 'lon')), parts along dimension 0
There are 2 independent parts, one for each index of `groups`. A program takes and returns all parts, laid end to end along the dimension named above; an argument that names none is the same for every part. Nothing has to cross between parts.
Inputs may be any that keep to these rules, and one draw needn't show every extreme that they name: level_ids holds each of 0 to 2 once.
All inputs are finite; a program needn't handle non-finite values.
Results may differ from a plain program's by a relative error of at most 0.014.
Values may be sent and summed in bfloat16 or wider, within the bound.
A program may use at most 128 MiB of HBM per device.

v0:
```python
import jax
import jax.numpy as jnp
from jax import lax
from jax.sharding import PartitionSpec as P

D = 512
HEADS = 8
PIN = 500
LEV = 3
LATL = 2
W_LAT = 4
W_LON = 8
STEPS = 2
ROW_PARTS = 4
norm_eps = 1e-05
head_eps = 1e-06


def product(einsum_form, left_side, right_side):
    return jnp.einsum(einsum_form, left_side, right_side, preferred_element_type=jnp.float32)


def layer_norm(values, scale_row):
    average = jnp.mean(values, axis=-1, keepdims=True)
    centred = values - average
    spread = jnp.mean(centred * centred, axis=-1, keepdims=True)
    return centred * lax.rsqrt(spread + norm_eps) * scale_row


def unit_heads(values):
    shaped = values.reshape(values.shape[:-1] + (HEADS, D // HEADS))
    mean_square = jnp.mean(shaped * shaped, axis=-1, keepdims=True)
    return (shaped * lax.rsqrt(mean_square + head_eps)).reshape(values.shape)


def level_tables(level_ids, level_embed, level_mix):
    picker = (level_ids[:, None] == jnp.arange(LEV, dtype=jnp.int32)[None, :]).astype(jnp.float32)
    embeds = jnp.dot(picker, level_embed.astype(jnp.float32), precision=lax.Precision.HIGHEST)
    mixing = jnp.dot(picker, level_mix, precision=lax.Precision.HIGHEST)
    return (embeds, mixing)


def head_tables(queries):
    head_dim = D // HEADS
    feature_head = jnp.arange(D, dtype=jnp.int32) // head_dim
    head_ids = jnp.arange(HEADS, dtype=jnp.int32)
    spreader = (head_ids[:, None] == feature_head[None, :]).astype(jnp.bfloat16)
    on_head = (feature_head[:, None] == head_ids[None, :]).astype(jnp.bfloat16)
    query_table = (queries.T[:, :, None] * on_head[:, None, :]).reshape(D, LATL * HEADS)
    return (query_table, spreader)


def encode(
    flat_fields,
    embeds,
    query_table,
    spreader,
    embed_weight,
    enc_gain,
    kv_weight,
    pool_out,
    latent_query,
):
    head_dim = D // HEADS
    patch_count = flat_fields.shape[0]
    patches = flat_fields.reshape(patch_count * LEV, PIN)
    tokens = jnp.dot(patches, embed_weight, preferred_element_type=jnp.float32).reshape(
        patch_count, LEV, D
    )
    tokens = layer_norm(tokens + embeds[None], enc_gain).astype(jnp.bfloat16)
    keyval = jnp.dot(
        tokens.reshape(patch_count * LEV, D), kv_weight, preferred_element_type=jnp.float32
    )
    key_rows = unit_heads(keyval[:, :D]).astype(jnp.bfloat16)
    value_rows = keyval[:, D:].astype(jnp.bfloat16).reshape(patch_count, LEV, 1, D)
    scores = jnp.dot(key_rows, query_table, preferred_element_type=jnp.float32) * head_dim ** (-0.5)
    scores = scores.reshape(patch_count, LEV, LATL * HEADS)
    weights = jnp.exp(scores)
    weights = (weights / jnp.sum(weights, axis=1, keepdims=True)).astype(jnp.bfloat16)
    spread_weights = jnp.dot(
        weights.reshape(patch_count * LEV * LATL, HEADS),
        spreader,
        preferred_element_type=jnp.float32,
    )
    spread_weights = spread_weights.reshape(patch_count, LEV, LATL, D)
    pooled = jnp.sum(spread_weights * value_rows.astype(jnp.float32), axis=1)
    pooled = pooled.astype(jnp.bfloat16).reshape(patch_count * LATL, D)
    latents = jnp.dot(pooled, pool_out, preferred_element_type=jnp.float32).reshape(
        patch_count, LATL, D
    )
    return (latents + latent_query.astype(jnp.float32)[None]).astype(jnp.bfloat16)


def increments(backbone_out, embeds, mixing, dec_gain, dec_weight):
    patch_count = backbone_out.shape[0]
    blended = mixing[None, :, 0, None] * backbone_out[:, None, 0, :].astype(jnp.float32)
    blended = blended + mixing[None, :, 1, None] * backbone_out[:, None, 1, :].astype(jnp.float32)
    blended = blended + embeds[None]
    normed = layer_norm(blended, dec_gain).astype(jnp.bfloat16)
    result = jnp.dot(
        normed.reshape(patch_count * LEV, D), dec_weight, preferred_element_type=jnp.float32
    )
    return result.astype(jnp.bfloat16).reshape(patch_count, LEV * PIN)


def window_block(shifted, attn_gain, qkv_weight, attn_proj):
    head_dim = D // HEADS
    lat_count, lon_count = (shifted.shape[0], shifted.shape[1])
    lat_win, lon_win = (lat_count // W_LAT, lon_count // W_LON)
    inside = W_LAT * W_LON * LATL
    flat_tokens = shifted.reshape(-1, D)
    normed = layer_norm(flat_tokens.astype(jnp.float32), attn_gain).astype(jnp.bfloat16)
    projected = jnp.dot(normed, qkv_weight, preferred_element_type=jnp.float32)
    query_heads = unit_heads(projected[:, :D]).astype(jnp.bfloat16)
    key_heads = unit_heads(projected[:, D : 2 * D]).astype(jnp.bfloat16)
    value_heads = projected[:, 2 * D :].astype(jnp.bfloat16)

    def to_windows(head_data):
        shaped = head_data.reshape(lat_win, W_LAT, lon_win, W_LON, LATL, HEADS, head_dim)
        return shaped.transpose(0, 2, 5, 1, 3, 4, 6).reshape(
            lat_win, lon_win, HEADS, inside, head_dim
        )

    scores = product(
        "abhqc,abhkc->abhqk", to_windows(query_heads), to_windows(key_heads)
    ) * head_dim ** (-0.5)
    row_index = jnp.arange(lat_count, dtype=jnp.int32).reshape(lat_win, W_LAT)
    region = (row_index >= lat_count - W_LAT // 2).astype(jnp.int32)
    region_tok = jnp.broadcast_to(region[:, :, None, None], (lat_win, W_LAT, W_LON, LATL)).reshape(
        lat_win, inside
    )
    allowed = (region_tok[:, :, None] == region_tok[:, None, :]).astype(jnp.float32)
    weights = jnp.exp(scores) * allowed[:, None, None, :, :]
    weights = (weights / jnp.sum(weights, axis=-1, keepdims=True)).astype(jnp.bfloat16)
    win_mix = product("abhqk,abhkc->abhqc", weights, to_windows(value_heads)).astype(jnp.bfloat16)
    win_mix = win_mix.reshape(lat_win, lon_win, HEADS, W_LAT, W_LON, LATL, head_dim)
    win_mix = win_mix.transpose(0, 3, 1, 4, 5, 2, 6).reshape(-1, D)
    attended = flat_tokens.astype(jnp.float32) + jnp.dot(
        win_mix, attn_proj, preferred_element_type=jnp.float32
    )
    return attended.astype(jnp.bfloat16).reshape(shifted.shape)


def mlp_block(restored, mlp_gain, mlp_up, mlp_down):
    flat_tokens = restored.reshape(-1, D)
    normed = layer_norm(flat_tokens.astype(jnp.float32), mlp_gain).astype(jnp.bfloat16)
    hidden = jax.nn.gelu(jnp.dot(normed, mlp_up, preferred_element_type=jnp.float32)).astype(
        jnp.bfloat16
    )
    result = flat_tokens.astype(jnp.float32) + jnp.dot(
        hidden, mlp_down, preferred_element_type=jnp.float32
    )
    return result.astype(jnp.bfloat16).reshape(restored.shape)


def shards(
    fields,
    level_ids,
    embed_weight,
    level_embed,
    enc_gain,
    latent_query,
    kv_weight,
    pool_out,
    attn_gain,
    qkv_weight,
    attn_proj,
    mlp_gain,
    mlp_up,
    mlp_down,
    level_mix,
    dec_gain,
    dec_weight,
):
    embeds, mixing = level_tables(level_ids, level_embed, level_mix)
    queries = unit_heads(latent_query.astype(jnp.float32)).astype(jnp.bfloat16)
    query_table, spreader = head_tables(queries)
    field_width = fields.shape[2]
    local_count = fields.shape[1]
    devices = lax.axis_size("lon")
    piece_cols = local_count // devices
    lat_count = devices // ROW_PARTS
    lon_dev = piece_cols * ROW_PARTS
    half_cols = W_LON // 2
    lag = half_cols // piece_cols
    piece = lax.axis_index("lon") // lat_count
    carry = (piece - lag) // ROW_PARTS
    latent_width = LATL * D
    current = fields
    for turn_index in range(STEPS):
        latents = encode(
            current.reshape(local_count, field_width),
            embeds,
            query_table,
            spreader,
            embed_weight,
            enc_gain,
            kv_weight,
            pool_out,
            latent_query,
        )
        blocks = latents.reshape(devices, piece_cols, latent_width)
        blocks = jnp.roll(blocks, carry, axis=0)
        got = lax.all_to_all(
            blocks.reshape(1, local_count, latent_width),
            "lon",
            split_axis=1,
            concat_axis=0,
            tiled=True,
        )
        tiles = got.reshape(ROW_PARTS, lat_count, piece_cols, latent_width).transpose(1, 0, 2, 3)
        tiles = jnp.roll(tiles, -lag, axis=1).reshape(lat_count, lon_dev, latent_width)
        tiles = jnp.roll(tiles, -(W_LAT // 2), axis=0).reshape(lat_count, lon_dev, LATL, D)
        attended = window_block(tiles, attn_gain, qkv_weight, attn_proj)
        backbone_out = mlp_block(attended, mlp_gain, mlp_up, mlp_down)
        values = backbone_out.reshape(lat_count, lon_dev, latent_width)
        extent = values.shape[2]
        values = jnp.roll(values, W_LAT // 2, axis=0)
        values = jnp.roll(values.reshape(lat_count, ROW_PARTS, piece_cols, extent), lag, axis=1)
        outgoing = values.transpose(1, 0, 2, 3).reshape(devices, piece_cols, extent)
        received = lax.all_to_all(outgoing, "lon", split_axis=0, concat_axis=1, tiled=True)
        home = received.reshape(devices, piece_cols, received.shape[2])
        home = jnp.roll(home, -carry, axis=0)
        home_latents = home.reshape(local_count, received.shape[2])
        added = increments(
            home_latents.reshape(local_count, LATL, D), embeds, mixing, dec_gain, dec_weight
        )
        added = added.reshape(current.shape)
        current = (current.astype(jnp.float32) + added.astype(jnp.float32)).astype(jnp.bfloat16)
    return current


def solution(mesh):
    placed = (
        P(("groups", "lon"), None, None),
        P("groups"),
        P(),
        P(),
        P(),
        P(),
        P(),
        P(),
        P(),
        P(),
        P(),
        P(),
        P(),
        P(),
        P(),
        P(),
        P(),
    )
    return jax.shard_map(
        shards,
        mesh=mesh,
        in_specs=placed,
        out_specs=P(("groups", "lon"), None, None),
        check_vma=False,
    )
```

profile of v0, /device:TPU:0, one launch (start us, length us, event | category | flops | bytes accessed | tf_op | source)
XLA Modules:
  0.0 169.1 jit_solution(9471271311963540494)
XLA Ops:
  0.6 1.1 dot_general.83
  2.5 1.3 fusion.138
  5.7 1.2 fusion.142
  7.6 1.8 %copy.290 = f32[96,512]{0,1:T(8,128)} copy(f32[96,512]{1,0:T(8,128)} %slice_multiply_fusion.1) | data formatting | bytes 393216 | tf_op jit(solution)/shard_map/mul | solution.py:32
  9.3 1.0 bitcast_reduce_fusion.1
  11.0 1.8 %copy.291 = f32[96,512]{1,0:T(8,128)} copy(f32[96,512]{0,1:T(8,128)} %bitcast.127) | data formatting | bytes 393216 | tf_op jit(solution)/shard_map/mul | solution.py:33
  13.5 1.3 convert_multiply_fusion
  14.8 1.4 mul.475
  16.1 1.4 reduce_sum.264
  18.8 1.4 mul.477
  21.5 1.7 fusion.17
  23.1 1.4 copy.292
  24.6 1.4 exp.32
  26.0 1.6 exp.31
  30.0 1.0 reshape.615
  31.1 0.9 divide_convert_fusion.5
  32.9 1.2 fusion.8
  35.1 1.0 reduce.8
  36.7 7.4 %all-to-all-start = ((bf16[16,2,1024]{2,1,0:T(2,128)(2,1)}), bf16[16,2,1024]{2,1,0:T(2,128)(2,1)}, u32[]{:S(2)}, u32[]{:S(2)}) async-start(bf16[16,2,1024]{2,1,0:T(2,128)(2,1)} %reshape.632), calls=%async_computation | async-start | bytes 131072 | tf_op jit(solution)/shard_map/all_to_all | solution.py:204
  45.2 1.0 add.248
  47.0 4.1 %all-to-all-done = bf16[16,2,1024]{2,1,0:T(2,128)(2,1)} async-done(((bf16[16,2,1024]{2,1,0:T(2,128)(2,1)}), bf16[16,2,1024]{2,1,0:T(2,128)(2,1)}, u32[]{:S(2)}, u32[]{:S(2)}) %all-to-all-start) | async-done | bytes 65568 | tf_op jit(solution)/shard_map/all_to_all | solution.py:204
  52.0 1.0 bitcast_reduce_fusion.3
  54.8 0.9 reshape.616
  56.0 1.9 %fusion.72 = f32[64,1536]{1,0:T(8,128)S(1)} fusion(bf16[512,1536]{1,0:T(8,128)(2,1)} %param.28, f32[64,512]{1,0:T(8,128)S(1)} %reshape.616, f32[512]{0:T(512)} %param.27, f32[64]{0:T(128)S(1)} %add_rsqrt_fusion.14, f32[64]{0:T(128)S(1)} %broadcast_multiply_fusion.7), kind=kOutput, calls=%fused_computation.140 | convolution fusion | flops 100794368 | bytes 2099712 | tf_op jit(solution)/shard_map/dot_general | solution.py:113
  59.4 1.7 %mul.492 = f32[64,8,64]{2,1,0:T(8,128)} reshape(f32[64,512]{1,0:T(8,128)} %get-tuple-element.13) | data formatting | bytes 262144 | tf_op jit(solution)/shard_map/mul | solution.py:32
  61.1 1.1 reduce_sum.269
  62.8 1.3 add_rsqrt_fusion.4
  65.7 1.7 %mul.494 = f32[64,512]{1,0:T(8,128)} reshape(f32[64,8,64]{2,1,0:T(8,128)} %mul.493) | data formatting | bytes 262144 | tf_op jit(solution)/shard_map/mul | solution.py:33
  67.4 1.7 %mul.497 = f32[64,8,64]{2,1,0:T(8,128)} reshape(f32[64,512]{1,0:T(8,128)} %get-tuple-element.12) | data formatting | bytes 262144 | tf_op jit(solution)/shard_map/mul | solution.py:32
  69.1 1.1 reduce_sum.270
  70.8 1.3 add_rsqrt_fusion.3
  73.7 1.7 %mul.499 = f32[64,512]{1,0:T(8,128)} reshape(f32[64,8,64]{2,1,0:T(8,128)} %mul.498) | data formatting | bytes 262144 | tf_op jit(solution)/shard_map/mul | solution.py:33
  75.4 1.8 %multiply_convert_fusion.11 = (bf16[64,512]{1,0:T(8,128)(2,1)}, bf16[64,512]{1,0:T(8,128)(2,1)}) fusion(f32[64,512]{1,0:T(8,128)} %mul.499, f32[64,1536]{1,0:T(8,128)} %copy-done.2, f32[64,512]{1,0:T(8,128)} %mul.494), kind=kLoop, calls=%fused_computation.112 | loop fusion | flops 131072 | bytes 655360 | tf_op jit(solution)/shard_map/convert_element_type | solution.py:115
  77.2 1.6 reshape.593
  78.8 1.7 copy.306
  80.5 1.6 reshape.595
  82.1 1.7 copy.309
  83.8 1.6 reshape.597
  85.4 1.7 copy.310
  87.0 1.9 %fusion.5 = f32[8,64,64]{1,2,0:T(8,128)} fusion(bf16[8,64,64]{2,1,0:T(8,128)(2,1)} %bitcast.136, bf16[8,64,64]{2,1,0:T(8,128)(2,1)} %bitcast.138, f32[64,64]{0,1:T(8,128)S(1)} %compare_convert_fusion), kind=kOutput, calls=%fused_computation.9 | convolution fusion | flops 4259840 | bytes 278528 | tf_op jit(solution)/shard_map/abhqc,abhkc->abhqk/dot_general | solution.py:20
  88.9 2.0 %convolution_convert_fusion.1 = bf16[8,64,64]{2,1,0:T(8,128)(2,1)} fusion(bf16[8,64,64]{2,1,0:T(8,128)(2,1)} %bitcast.153, f32[8,64,64]{1,2,0:T(8,128)} %fusion.5), kind=kOutput, calls=%fused_computation.13 | convolution fusion | flops 4293183 | bytes 262144 | tf_op jit(solution)/shard_map/abhqk,abhkc->abhqc/dot_general | solution.py:20
  90.9 1.7 %copy.396 = bf16[1,1,8,4,8,2,64]{6,2,5,4,3,1,0:T(8,128)(2,1)} copy(bf16[1,1,8,4,8,2,64]{6,5,4,3,2,1,0:T(2,128)(2,1)} %bitcast.154) | data formatting | bytes 131072 | tf_op jit(solution)/shard_map/reshape | solution.py:136
  92.6 1.1 reshape.600
  93.6 1.4 fusion.139
  95.9 2.6 %fusion.11 = bf16[64,512]{1,0:T(8,128)(2,1)S(1)} fusion(f32[64,512]{1,0:T(8,128)} %copy-done.8, bf16[2048,512]{1,0:T(8,128)(2,1)S(1)} %copy-done, bf16[512,2048]{1,0:T(8,128)(2,1)} %param.31, f32[512]{0:T(512)} %param.30, f32[64]{0:T(128)S(1)} %add_rsqrt_fusion.13, f32[64]{0:T(128)S(1)} %broadcast_multiply_fusion.6), kind=kOutput, calls=%fused_computation.27 | convolution fusion | flops 269811712 | bytes 4393472 | tf_op jit(solution)/shard_map/dot_general | solution.py:150
  99.5 3.5 %all-to-all-start.1 = ((bf16[16,2,1024]{2,1,0:T(2,128)(2,1)}), bf16[16,2,1024]{2,1,0:T(2,128)(2,1)S(1)}, u32[]{:S(2)}, u32[]{:S(2)}) async-start(bf16[16,2,1024]{2,1,0:T(2,128)(2,1)} %bitcast.22), calls=%async_computation.1 | async-start | bytes 131072 | tf_op jit(solution)/shard_map/all_to_all | solution.py:221
  104.3 5.5 %all-to-all-done.1 = bf16[16,2,1024]{2,1,0:T(2,128)(2,1)S(1)} async-done(((bf16[16,2,1024]{2,1,0:T(2,128)(2,1)}), bf16[16,2,1024]{2,1,0:T(2,128)(2,1)S(1)}, u32[]{:S(2)}, u32[]{:S(2)}) %all-to-all-start.1) | async-done | bytes 65568 | tf_op jit(solution)/shard_map/all_to_all | solution.py:221
  113.1 1.7 %mul.516 = f32[96,512]{1,0:T(8,128)} reshape(f32[32,3,512]{2,1,0:T(4,128)} %mul.515.clone) | data formatting | bytes 393216 | tf_op jit(solution)/shard_map/mul | solution.py:96
  115.5 1.7 %mul.525 = f32[96,512]{1,0:T(8,128)} reshape(f32[32,3,512]{2,1,0:T(4,128)} %mul.524.clone) | data formatting | bytes 393216 | tf_op jit(solution)/shard_map/mul | solution.py:97
  117.3 2.2 %fusion.6 = f32[96,500]{1,0:T(8,128)} fusion(bf16[512,500]{0,1:T(8,128)(2,1)} %param.35, f32[96,512]{1,0:T(8,128)S(1)} %add.248, f32[96,512]{1,0:T(8,128)} %mul.525, f32[96,512]{1,0:T(8,128)} %mul.516, f32[512]{0:T(512)} %param.34, f32[96]{0:T(128)S(1)} %rsqrt.134, f32[96]{0:T(128)S(1)} %div.166, f32[96]{0:T(128)} %mul.520, f32[96]{0:T(128)} %mul.462), kind=kOutput, calls=%fused_computation.16 | convolution fusion | flops 49641216 | bytes 1297408 | tf_op jit(solution)/shard_map/dot_general | solution.py:100
  119.5 1.0 reshape.619
  120.5 0.9 add_convert_fusion.1
  121.6 1.3 fusion.140
  124.1 1.2 fusion.143
  127.8 0.9 divide_convert_fusion.4
  130.9 1.0 reduce.9
  131.9 9.7 %all_to_all.16 = bf16[16,2,1024]{2,1,0:T(2,128)(2,1)S(1)} all-to-all(bf16[16,2,1024]{2,1,0:T(2,128)(2,1)S(1)} %reshape.634), channel_id=1, replica_groups=mesh['groups'=2,'lon'=16] {'lon'}, dimensions={0} | all-to-all | bytes 131072 | tf_op jit(solution)/shard_map/all_to_all | solution.py:204
  142.6 1.8 %fusion.74 = f32[64,1536]{1,0:T(8,128)S(1)} fusion(bf16[512,1536]{1,0:T(8,128)(2,1)} %param.28, f32[64,512]{1,0:T(8,128)S(1)} %reshape.621, f32[64]{0:T(128)S(1)} %add_rsqrt_fusion.12, f32[64]{0:T(128)S(1)} %broadcast_multiply_fusion.5, f32[512]{0:T(512)S(1)} %copy-done.20), kind=kOutput, calls=%fused_computation.142 | convolution fusion | flops 100794368 | bytes 2099712 | tf_op jit(solution)/shard_map/dot_general | solution.py:113
  147.2 1.0 reshape.606
  148.5 1.0 reshape.610
  150.5 1.2 convolution_convert_fusion
  152.5 2.5 %fusion.15 = bf16[64,512]{1,0:T(8,128)(2,1)S(1)} fusion(f32[64,512]{1,0:T(8,128)S(1)} %get-tuple-element.43, bf16[2048,512]{1,0:T(8,128)(2,1)S(1)} %copy-done, bf16[512,2048]{1,0:T(8,128)(2,1)} %param.31, f32[64]{0:T(128)S(1)} %add_rsqrt_fusion.11, f32[64]{0:T(128)S(1)} %broadcast_multiply_fusion.4, f32[512]{0:T(512)S(1)} %copy-done.21), kind=kOutput, calls=%fused_computation.31 | convolution fusion | flops 269811712 | bytes 4393472 | tf_op jit(solution)/shard_map/dot_general | solution.py:150
  155.4 9.5 %all_to_all.17 = bf16[16,2,1024]{2,1,0:T(2,128)(2,1)S(1)} all-to-all(bf16[16,2,1024]{2,1,0:T(2,128)(2,1)S(1)} %bitcast.151), channel_id=1, replica_groups=mesh['groups'=2,'lon'=16] {'lon'}, dimensions={0} | all-to-all | bytes 131072 | tf_op jit(solution)/shard_map/all_to_all | solution.py:221
  167.1 1.2 fusion.7
  (241 shorter events, 45.1 us)
Async XLA Ops:
  0.0 95.8 %copy-start = (bf16[2048,512]{1,0:T(8,128)(2,1)S(1)}, bf16[2048,512]{1,0:T(8,128)(2,1)}, u32[]{:S(2)}) copy-start(bf16[2048,512]{1,0:T(8,128)(2,1)} %param.32) | copy-start | bytes 6291460
  0.0 5.7 %copy-start.1 = (bf16[512,1024]{1,0:T(8,128)(2,1)S(1)}, bf16[512,1024]{1,0:T(8,128)(2,1)}, u32[]{:S(2)}) copy-start(bf16[512,1024]{1,0:T(8,128)(2,1)} %param.25) | copy-start | bytes 3145732
  20.9 0.6 copy-start.18
  28.2 18.0 %copy-start.26 = (f32[3,2]{0,1:T(2,128)S(1)}, f32[3,2]{0,1:T(2,128)}, u32[]{:S(2)}) copy-start(f32[3,2]{0,1:T(2,128)} %param.33) | copy-start | bytes 76
  28.2 18.0 %copy-start.27 = (s32[3]{0:T(128)S(1)}, s32[3]{0:T(128)}, u32[]{:S(2)}) copy-start(s32[3]{0:T(128)} %param.20) | copy-start | bytes 40
  28.9 15.5 %copy-start.13 = (f32[2,512]{1,0:T(2,128)}, f32[2,512]{1,0:T(2,128)S(1)}, u32[]{:S(2)}) copy-start(f32[2,512]{1,0:T(2,128)S(1)} %convert_element_type.247) | copy-start | bytes 12292
  36.7 14.4 %all-to-all-start = ((bf16[16,2,1024]{2,1,0:T(2,128)(2,1)}), bf16[16,2,1024]{2,1,0:T(2,128)(2,1)}, u32[]{:S(2)}, u32[]{:S(2)}) async-start(bf16[16,2,1024]{2,1,0:T(2,128)(2,1)} %reshape.632), calls=%async_computation | async-start | bytes 131072 | tf_op jit(solution)/shard_map/all_to_all | solution.py:204
  44.4 42.6 %copy-start.11 = (f32[64,64]{0,1:T(8,128)}, f32[64,64]{0,1:T(8,128)S(1)}, u32[]{:S(2)}) copy-start(f32[64,64]{0,1:T(8,128)S(1)} %compare_convert_fusion) | copy-start | bytes 49156
  46.3 71.0 %copy-start.6 = (f32[96,512]{1,0:T(8,128)}, f32[96,512]{1,0:T(8,128)S(1)}, u32[]{:S(2)}) copy-start(f32[96,512]{1,0:T(8,128)S(1)} %add.248) | copy-start | bytes 589828
  57.9 0.8 copy-start.2
  95.0 0.6 copy-start.8
  95.8 7.1 %copy-start.25 = (f32[3,2]{0,1:T(2,128)S(1)}, f32[3,2]{0,1:T(2,128)}, u32[]{:S(2)}) copy-start(f32[3,2]{0,1:T(2,128)} %fusion.118) | copy-start | bytes 76
  99.5 10.4 %all-to-all-start.1 = ((bf16[16,2,1024]{2,1,0:T(2,128)(2,1)}), bf16[16,2,1024]{2,1,0:T(2,128)(2,1)S(1)}, u32[]{:S(2)}, u32[]{:S(2)}) async-start(bf16[16,2,1024]{2,1,0:T(2,128)(2,1)} %bitcast.22), calls=%async_computation.1 | async-start | bytes 131072 | tf_op jit(solution)/shard_map/all_to_all | solution.py:221
  103.0 6.8 %copy-start.14 = (f32[3]{0:T(128)}, f32[3]{0:T(128)S(1)}, u32[]{:S(2)}) copy-start(f32[3]{0:T(128)S(1)} %get-tuple-element.34) | copy-start | bytes 40
  103.0 6.8 %copy-start.16 = (f32[3]{0:T(128)}, f32[3]{0:T(128)S(1)}, u32[]{:S(2)}) copy-start(f32[3]{0:T(128)S(1)} %get-tuple-element.35) | copy-start | bytes 40
  114.8 8.4 %copy-start.19 = (f32[512]{0:T(512)S(1)}, f32[512]{0:T(512)}, u32[]{:S(2)}) copy-start(f32[512]{0:T(512)} %param.23) | copy-start | bytes 6148
  121.4 1.9 %copy-start.9 = (bf16[1,32,1500]{2,1,0:T(8,128)(2,1)}, bf16[1,32,1500]{2,1,0:T(8,128)(2,1)S(1)}, u32[]{:S(2)}) copy-start(bf16[1,32,1500]{2,1,0:T(8,128)(2,1)S(1)} %add_convert_fusion.1) | copy-start | bytes 288004
  125.3 4.3 %copy-start.3 = (bf16[512,512]{1,0:T(8,128)(2,1)S(1)}, bf16[512,512]{1,0:T(8,128)(2,1)}, u32[]{:S(2)}) copy-start(bf16[512,512]{1,0:T(8,128)(2,1)} %param.26) | copy-start | bytes 1572868
  127.8 14.9 %copy-start.20 = (f32[512]{0:T(512)S(1)}, f32[512]{0:T(512)}, u32[]{:S(2)}) copy-start(f32[512]{0:T(512)} %param.27) | copy-start | bytes 6148
  145.6 4.7 %copy-start.12 = (f32[64,64]{0,1:T(8,128)S(1)}, f32[64,64]{0,1:T(8,128)}, u32[]{:S(2)}) copy-start(f32[64,64]{0,1:T(8,128)} %copy-done.11) | copy-start | bytes 49156
  146.5 5.4 %copy-start.4 = (bf16[512,512]{1,0:T(8,128)(2,1)S(1)}, bf16[512,512]{1,0:T(8,128)(2,1)}, u32[]{:S(2)}) copy-start(bf16[512,512]{1,0:T(8,128)(2,1)} %param.29) | copy-start | bytes 1572868
  148.1 4.3 %copy-start.21 = (f32[512]{0:T(512)S(1)}, f32[512]{0:T(512)}, u32[]{:S(2)}) copy-start(f32[512]{0:T(512)} %param.30) | copy-start | bytes 6148
  152.5 12.8 %copy-start.15 = (f32[3]{0:T(128)S(1)}, f32[3]{0:T(128)}, u32[]{:S(2)}) copy-start(f32[3]{0:T(128)} %copy-done.14) | copy-start | bytes 40
  152.5 12.8 %copy-start.17 = (f32[3]{0:T(128)S(1)}, f32[3]{0:T(128)}, u32[]{:S(2)}) copy-start(f32[3]{0:T(128)} %copy-done.16) | copy-start | bytes 40
  155.0 12.1 %copy-start.5 = (bf16[512,500]{0,1:T(8,128)(2,1)S(1)}, bf16[512,500]{0,1:T(8,128)(2,1)}, u32[]{:S(2)}) copy-start(bf16[512,500]{0,1:T(8,128)(2,1)} %param.35) | copy-start | bytes 1536004
  155.0 12.1 %copy-start.7 = (f32[96,512]{1,0:T(8,128)S(1)}, f32[96,512]{1,0:T(8,128)}, u32[]{:S(2)}) copy-start(f32[96,512]{1,0:T(8,128)} %copy-done.6) | copy-start | bytes 589828
  155.0 12.1 %copy-start.22 = (f32[512]{0:T(512)S(1)}, f32[512]{0:T(512)}, u32[]{:S(2)}) copy-start(f32[512]{0:T(512)} %param.34) | copy-start | bytes 6148
  155.0 12.1 %copy-start.23 = (f32[96]{0:T(128)S(1)}, f32[96]{0:T(128)}, u32[]{:S(2)}) copy-start(f32[96]{0:T(128)} %mul.462) | copy-start | bytes 1156
  155.1 12.0 %copy-start.24 = (f32[96]{0:T(128)S(1)}, f32[96]{0:T(128)}, u32[]{:S(2)}) copy-start(f32[96]{0:T(128)} %mul.520) | copy-start | bytes 1156
  165.1 3.3 %copy-start.10 = (bf16[1,32,1500]{2,1,0:T(8,128)(2,1)S(1)}, bf16[1,32,1500]{2,1,0:T(8,128)(2,1)}, u32[]{:S(2)}) copy-start(bf16[1,32,1500]{2,1,0:T(8,128)(2,1)} %copy-done.9) | copy-start | bytes 288004
where the time goes:
time: 172 us; the launch traced here: 169 us
  local copies, waits for them, and re-layouts  66.6 us (39%)
  matrix products  32.2 us (19%)
  other arithmetic  29.3 us (17%)
  blocking collectives  19.1 us (11%)
  starting transfers between devices  10.9 us (6%)
  waiting for transfers between devices  9.6 us (6%)
    mul x14, local copies, waits for them, and re-layouts, unit_heads(): return (shaped * lax.rsqrt(mean_square + head_eps)).reshape(values.shape)  10.2 us
    all_to_all x1, blocking collectives, shards(): lax.all_to_all(blocks.reshape(1, local_count, latent_width), 'lon', split...  9.66 us
    all_to_all x1, blocking collectives, shards(): lax.all_to_all(outgoing, 'lon', split_axis=0, concat_axis=1, tiled=True)  9.48 us
    all_to_all x1, starting transfers between devices, shards(): lax.all_to_all(blocks.reshape(1, local_count, latent_width), 'lon', split...  7.44 us
    reshape x6, local copies, waits for them, and re-layouts, to_windows(): head_data.reshape(lat_win, W_LAT, lon_win, W_LON, LATL, HEADS, head_dim)  6.95 us
    mul x7, local copies, waits for them, and re-layouts, unit_heads(): mean_square = jnp.mean(shaped * shaped, axis=-1, keepdims=True)  6.84 us
    transpose x6, local copies, waits for them, and re-layouts, to_windows(): shaped.transpose(0, 2, 5, 1, 3, 4, 6)  5.92 us
    all_to_all x1, waiting for transfers between devices, shards(): lax.all_to_all(outgoing, 'lon', split_axis=0, concat_axis=1, tiled=True)  5.53 us
  transfers between devices with their start and end apart: 2, of which 2 were waited for; matrix products, arithmetic and copies ran while one was open for 2% of the time, Pallas kernels for 0%

commit v1 on v0

--- a/solution.py
+++ b/solution.py
@@ -218,7 +218,19 @@
         values = jnp.roll(values, W_LAT // 2, axis=0)
         values = jnp.roll(values.reshape(lat_count, ROW_PARTS, piece_cols, extent), lag, axis=1)
         outgoing = values.transpose(1, 0, 2, 3).reshape(devices, piece_cols, extent)
-        received = lax.all_to_all(outgoing, "lon", split_axis=0, concat_axis=1, tiled=True)
+        ways, here = (lax.axis_size("lon"), lax.axis_index("lon"))
+        width = outgoing.shape[0] // ways
+        dims = list(outgoing.shape)
+        dims[0] = width
+        height = dims[1]
+        dims[1] = height * ways
+        full = jnp.zeros(dims, outgoing.dtype)
+        for mask in range(ways):
+            part = lax.dynamic_slice_in_dim(outgoing, (here ^ mask) * width, width, axis=0)
+            if mask:
+                part = lax.ppermute(part, "lon", [(d, d ^ mask) for d in range(ways)])
+            full = lax.dynamic_update_slice_in_dim(full, part, (here ^ mask) * height, axis=1)
+        received = full
         home = received.reshape(devices, piece_cols, received.shape[2])
         home = jnp.roll(home, -carry, axis=0)
         home_latents = home.reshape(local_count, received.shape[2])

time: 172 us -> 187 us (1.087)
  starting transfers between devices: 10.9 us -> 49.4 us
  local copies, waits for them, and re-layouts: 66.6 us -> 54.7 us
  blocking collectives: 19.1 us -> 12.2 us
  other arithmetic: 29.3 us -> 26.7 us
    ppermute x0 -> x30, starting transfers between devices: none -> 42.1 us  [shards(): part = lax.ppermute(part, 'lon', [(d, d ^ mask) for d in range(ways)])]
    all_to_all x1 -> x0, blocking collectives: 9.48 us -> none  [shards(): lax.all_to_all(outgoing, 'lon', split_axis=0, concat_axis=1, tiled=True)]
    all_to_all x1 -> x0, waiting for transfers between devices: 5.53 us -> none  [shards(): lax.all_to_all(outgoing, 'lon', split_axis=0, concat_axis=1, tiled=True)]
    ppermute x0 -> x30, waiting for transfers between devices: none -> 3.75 us  [shards(): part = lax.ppermute(part, 'lon', [(d, d ^ mask) for d in range(ways)])]
    all_to_all x1 -> x0, starting transfers between devices: 3.5 us -> none  [shards(): lax.all_to_all(outgoing, 'lon', split_axis=0, concat_axis=1, tiled=True)]
    rsqrt x7, other arithmetic: 3.25 us -> 0.73 us  [unit_heads(): return (shaped * lax.rsqrt(mean_square + head_eps)).reshape(values.shape)]
    all_to_all x1, blocking collectives: 9.66 us -> 12.2 us  [shards(): lax.all_to_all(blocks.reshape(1, local_count, latent_width), 'lon', split...]
    transpose x6, local copies, waits for them, and re-layouts: 5.92 us -> 3.72 us  [to_windows(): shaped.transpose(0, 2, 5, 1, 3, 4, 6)]
  transfers between devices with their start and end apart: 2 -> 31, of which waited for: 2 -> 5; matrix products, arithmetic and copies ran while one was open for 2% -> 3% of each run, Pallas kernels for 0% -> 0%
where the time goes in v1:
time: 187 us; the launch traced here: 184 us
  local copies, waits for them, and re-layouts  54.7 us (29%)
  starting transfers between devices  49.4 us (26%)
  matrix products  30.6 us (16%)
  other arithmetic  26.7 us (14%)
  blocking collectives  12.2 us (7%)
  waiting for transfers between devices  8.93 us (5%)
    ppermute x30, starting transfers between devices, shards(): part = lax.ppermute(part, 'lon', [(d, d ^ mask) for d in range(ways)])  42.1 us
    all_to_all x1, blocking collectives, shards(): lax.all_to_all(blocks.reshape(1, local_count, latent_width), 'lon', split...  12.2 us
    mul x14, local copies, waits for them, and re-layouts, unit_heads(): return (shaped * lax.rsqrt(mean_square + head_eps)).reshape(values.shape)  8.44 us
    all_to_all x1, starting transfers between devices, shards(): lax.all_to_all(blocks.reshape(1, local_count, latent_width), 'lon', split...  7.39 us
    reshape x6, local copies, waits for them, and re-layouts, to_windows(): head_data.reshape(lat_win, W_LAT, lon_win, W_LON, LATL, HEADS, head_dim)  5.45 us
    mul x7, local copies, waits for them, and re-layouts, unit_heads(): mean_square = jnp.mean(shaped * shaped, axis=-1, keepdims=True)  5.44 us
    exp x6, local copies, waits for them, and re-layouts, encode(): weights = jnp.exp(scores)  5.27 us
    all_to_all x1, waiting for transfers between devices, shards(): lax.all_to_all(blocks.reshape(1, local_count, latent_width), 'lon', split...  5.18 us
  transfers between devices with their start and end apart: 31, of which 5 were waited for; matrix products, arithmetic and copies ran while one was open for 3% of the time, Pallas kernels for 0%

profile of v1, /device:TPU:0, one launch (start us, length us, event | category | flops | bytes accessed | tf_op | source)
XLA Modules:
  0.0 184.4 jit_solution(11444246375895191884)
XLA Ops:
  0.6 1.1 dot_general.83
  2.5 1.3 fusion.138
  5.7 1.2 fusion.142
  7.6 1.8 copy.290
  9.4 1.0 bitcast_reduce_fusion.1
  11.1 1.8 copy.291
  13.5 1.3 convert_multiply_fusion
  14.8 1.4 mul.539
  16.1 1.4 reduce_sum.264
  18.9 1.4 mul.541
  21.5 1.7 fusion.17
  23.2 1.4 copy.292
  24.6 1.4 exp.32
  26.0 1.6 exp.31
  30.0 1.0 reshape.613
  31.1 0.9 divide_convert_fusion.5
  33.0 1.2 fusion.8
  35.2 1.0 reduce.8
  36.8 7.4 %all-to-all-start = ((bf16[16,2,1024]{2,1,0:T(2,128)(2,1)}), bf16[16,2,1024]{2,1,0:T(2,128)(2,1)S(1)}, u32[]{:S(2)}, u32[]{:S(2)}) async-start(bf16[16,2,1024]{2,1,0:T(2,128)(2,1)} %reshape.630), calls=%async_computation | async-start | bytes 131072 | tf_op jit(solution)/shard_map/all_to_all | solution.py:204
  45.9 5.2 %all-to-all-done = bf16[16,2,1024]{2,1,0:T(2,128)(2,1)S(1)} async-done(((bf16[16,2,1024]{2,1,0:T(2,128)(2,1)}), bf16[16,2,1024]{2,1,0:T(2,128)(2,1)S(1)}, u32[]{:S(2)}, u32[]{:S(2)}) %all-to-all-start) | async-done | bytes 65568 | tf_op jit(solution)/shard_map/all_to_all | solution.py:204
  52.2 1.8 fusion.72
  55.5 1.0 mul.556
  60.5 1.0 mul.561
  65.4 1.7 multiply_convert_fusion.11
  67.4 1.6 reshape.591
  69.0 1.0 copy.309
  70.0 1.6 reshape.593
  71.6 1.7 copy.310
  73.3 1.7 fusion.5
  75.0 1.3 convolution_convert_fusion.1
  76.6 1.4 fusion.139
  78.2 2.6 %fusion.11 = bf16[64,512]{1,0:T(8,128)(2,1)S(1)} fusion(f32[64,512]{1,0:T(8,128)S(1)} %get-tuple-element.71, bf16[2048,512]{1,0:T(8,128)(2,1)S(1)} %copy-done, bf16[512,2048]{1,0:T(8,128)(2,1)} %param.31, f32[512]{0:T(512)} %param.30, f32[64]{0:T(128)S(1)} %add_rsqrt_fusion.13, f32[64]{0:T(128)S(1)} %broadcast_multiply_fusion.6), kind=kOutput, calls=%fused_computation.27 | convolution fusion | flops 269811712 | bytes 4393472 | tf_op jit(solution)/shard_map/dot_general | solution.py:150
  82.2 1.0 add.408
  84.7 1.6 collective-permute-start.2
  86.4 1.7 collective-permute-start.4
  88.3 2.4 %collective-permute-start.6 = (bf16[1,2,1024]{2,1,0:T(2,128)(2,1)S(1)}, bf16[1,2,1024]{2,1,0:T(2,128)(2,1)S(1)}, u32[]{:S(2)}, u32[]{:S(2)}) collective-permute-start(bf16[1,2,1024]{2,1,0:T(2,128)(2,1)S(1)} %get-tuple-element.50), channel_id=1, source_target_pairs={{0,7},{1,6},{2,5},{3,4},{4,3},{5,2},{6,1},{7,0},{8,15},{9,14},{10,... | collective-permute-start | bytes 12296 | tf_op jit(solution)/shard_map/ppermute | solution.py:231
  91.1 2.5 %collective-permute-start.8 = (bf16[1,2,1024]{2,1,0:T(2,128)(2,1)S(1)}, bf16[1,2,1024]{2,1,0:T(2,128)(2,1)S(1)}, u32[]{:S(2)}, u32[]{:S(2)}) collective-permute-start(bf16[1,2,1024]{2,1,0:T(2,128)(2,1)S(1)} %get-tuple-element.48), channel_id=1, source_target_pairs={{0,9},{1,8},{2,11},{3,10},{4,13},{5,12},{6,15},{7,14},{8,1},{9,0},... | collective-permute-start | bytes 12296 | tf_op jit(solution)/shard_map/ppermute | solution.py:231
  94.1 3.3 %collective-permute-start.10 = (bf16[1,2,1024]{2,1,0:T(2,128)(2,1)S(1)}, bf16[1,2,1024]{2,1,0:T(2,128)(2,1)S(1)}, u32[]{:S(2)}, u32[]{:S(2)}) collective-permute-start(bf16[1,2,1024]{2,1,0:T(2,128)(2,1)S(1)} %get-tuple-element.46), channel_id=1, source_target_pairs={{0,11},{1,10},{2,9},{3,8},{4,15},{5,14},{6,13},{7,12},{8,3},{9,2},... | collective-permute-start | bytes 12296 | tf_op jit(solution)/shard_map/ppermute | solution.py:231
  98.0 3.1 %collective-permute-start.12 = (bf16[1,2,1024]{2,1,0:T(2,128)(2,1)S(1)}, bf16[1,2,1024]{2,1,0:T(2,128)(2,1)S(1)}, u32[]{:S(2)}, u32[]{:S(2)}) collective-permute-start(bf16[1,2,1024]{2,1,0:T(2,128)(2,1)S(1)} %get-tuple-element.44), channel_id=1, source_target_pairs={{0,13},{1,12},{2,15},{3,14},{4,9},{5,8},{6,11},{7,10},{8,5},{9,4},... | collective-permute-start | bytes 12296 | tf_op jit(solution)/shard_map/ppermute | solution.py:231
  101.8 3.8 %collective-permute-start.14 = (bf16[1,2,1024]{2,1,0:T(2,128)(2,1)S(1)}, bf16[1,2,1024]{2,1,0:T(2,128)(2,1)S(1)}, u32[]{:S(2)}, u32[]{:S(2)}) collective-permute-start(bf16[1,2,1024]{2,1,0:T(2,128)(2,1)S(1)} %get-tuple-element.42), channel_id=1, source_target_pairs={{0,15},{1,14},{2,13},{3,12},{4,11},{5,10},{6,9},{7,8},{8,7},{9,6},... | collective-permute-start | bytes 12296 | tf_op jit(solution)/shard_map/ppermute | solution.py:231
  105.8 1.7 collective-permute-done.13
  111.9 1.7 mul.596
  114.3 1.0 mul.605
  115.4 2.2 %fusion.6 = f32[96,500]{1,0:T(8,128)} fusion(bf16[512,500]{0,1:T(8,128)(2,1)} %param.35, f32[96,512]{1,0:T(8,128)S(1)} %add.408, f32[96,512]{1,0:T(8,128)S(1)} %mul.605, f32[96,512]{1,0:T(8,128)} %mul.596, f32[512]{0:T(512)} %param.34, f32[96]{0:T(128)} %rsqrt.134, f32[96]{0:T(128)} %div.166, f32[96]{0:T(128)} %mul.600, f32[96]{0:T(128)} %mul.526), kind=kOutput, calls=%fused_computation.16 | convolution fusion | flops 49641216 | bytes 1297408 | tf_op jit(solution)/shard_map/dot_general | solution.py:100
  117.5 1.0 reshape.617
  119.7 1.3 fusion.140
  122.8 1.2 fusion.143
  126.5 0.9 divide_convert_fusion.4
  129.6 1.0 reduce.9
  130.6 12.2 %all_to_all.8 = bf16[16,2,1024]{2,1,0:T(2,128)(2,1)S(1)} all-to-all(bf16[16,2,1024]{2,1,0:T(2,128)(2,1)S(1)} %reshape.632), channel_id=1, replica_groups=mesh['groups'=2,'lon'=16] {'lon'}, dimensions={0} | all-to-all | bytes 131072 | tf_op jit(solution)/shard_map/all_to_all | solution.py:204
  143.9 1.8 fusion.74
  148.4 1.0 reshape.603
  149.8 1.0 reshape.607
  151.7 1.2 convolution_convert_fusion
  153.7 2.5 %fusion.15 = bf16[64,512]{1,0:T(8,128)(2,1)S(1)} fusion(f32[64,512]{1,0:T(8,128)S(1)} %get-tuple-element.75, bf16[2048,512]{1,0:T(8,128)(2,1)S(1)} %copy-done, bf16[512,2048]{1,0:T(8,128)(2,1)} %param.31, f32[64]{0:T(128)S(1)} %add_rsqrt_fusion.11, f32[64]{0:T(128)S(1)} %broadcast_multiply_fusion.4, f32[512]{0:T(512)S(1)} %copy-done.19), kind=kOutput, calls=%fused_computation.31 | convolution fusion | flops 269811712 | bytes 4393472 | tf_op jit(solution)/shard_map/dot_general | solution.py:150
  157.1 1.6 collective-permute-start.17
  158.9 1.5 collective-permute-start.19
  160.7 2.5 %collective-permute-start.21 = (bf16[1,2,1024]{2,1,0:T(2,128)(2,1)S(1)}, bf16[1,2,1024]{2,1,0:T(2,128)(2,1)S(1)}, u32[]{:S(2)}, u32[]{:S(2)}) collective-permute-start(bf16[1,2,1024]{2,1,0:T(2,128)(2,1)S(1)} %get-tuple-element.24), channel_id=1, source_target_pairs={{0,7},{1,6},{2,5},{3,4},{4,3},{5,2},{6,1},{7,0},{8,15},{9,14},{10,... | collective-permute-start | bytes 12296 | tf_op jit(solution)/shard_map/ppermute | solution.py:231
  163.6 2.4 %collective-permute-start.23 = (bf16[1,2,1024]{2,1,0:T(2,128)(2,1)S(1)}, bf16[1,2,1024]{2,1,0:T(2,128)(2,1)S(1)}, u32[]{:S(2)}, u32[]{:S(2)}) collective-permute-start(bf16[1,2,1024]{2,1,0:T(2,128)(2,1)S(1)} %get-tuple-element.22), channel_id=1, source_target_pairs={{0,9},{1,8},{2,11},{3,10},{4,13},{5,12},{6,15},{7,14},{8,1},{9,0},... | collective-permute-start | bytes 12296 | tf_op jit(solution)/shard_map/ppermute | solution.py:231
  166.5 3.3 %collective-permute-start.25 = (bf16[1,2,1024]{2,1,0:T(2,128)(2,1)S(1)}, bf16[1,2,1024]{2,1,0:T(2,128)(2,1)S(1)}, u32[]{:S(2)}, u32[]{:S(2)}) collective-permute-start(bf16[1,2,1024]{2,1,0:T(2,128)(2,1)S(1)} %get-tuple-element.20), channel_id=1, source_target_pairs={{0,11},{1,10},{2,9},{3,8},{4,15},{5,14},{6,13},{7,12},{8,3},{9,2},... | collective-permute-start | bytes 12296 | tf_op jit(solution)/shard_map/ppermute | solution.py:231
  170.4 3.0 %collective-permute-start.27 = (bf16[1,2,1024]{2,1,0:T(2,128)(2,1)S(1)}, bf16[1,2,1024]{2,1,0:T(2,128)(2,1)S(1)}, u32[]{:S(2)}, u32[]{:S(2)}) collective-permute-start(bf16[1,2,1024]{2,1,0:T(2,128)(2,1)S(1)} %get-tuple-element.18), channel_id=1, source_target_pairs={{0,13},{1,12},{2,15},{3,14},{4,9},{5,8},{6,11},{7,10},{8,5},{9,4},... | collective-permute-start | bytes 12296 | tf_op jit(solution)/shard_map/ppermute | solution.py:231
  174.3 3.8 %collective-permute-start.29 = (bf16[1,2,1024]{2,1,0:T(2,128)(2,1)S(1)}, bf16[1,2,1024]{2,1,0:T(2,128)(2,1)S(1)}, u32[]{:S(2)}, u32[]{:S(2)}) collective-permute-start(bf16[1,2,1024]{2,1,0:T(2,128)(2,1)S(1)} %get-tuple-element.16), channel_id=1, source_target_pairs={{0,15},{1,14},{2,13},{3,12},{4,11},{5,10},{6,9},{7,8},{8,7},{9,6},... | collective-permute-start | bytes 12296 | tf_op jit(solution)/shard_map/ppermute | solution.py:231
  178.3 1.6 collective-permute-done.28
  182.4 1.2 fusion.7
  (328 shorter events, 55.6 us)
Async XLA Ops:
  0.0 78.2 %copy-start = (bf16[2048,512]{1,0:T(8,128)(2,1)S(1)}, bf16[2048,512]{1,0:T(8,128)(2,1)}, u32[]{:S(2)}) copy-start(bf16[2048,512]{1,0:T(8,128)(2,1)} %param.32) | copy-start | bytes 6291460
  0.0 5.7 %copy-start.1 = (bf16[512,1024]{1,0:T(8,128)(2,1)S(1)}, bf16[512,1024]{1,0:T(8,128)(2,1)}, u32[]{:S(2)}) copy-start(bf16[512,1024]{1,0:T(8,128)(2,1)} %param.25) | copy-start | bytes 3145732
  20.9 0.6 copy-start.16
  28.3 16.9 %copy-start.23 = (f32[3,2]{0,1:T(2,128)S(1)}, f32[3,2]{0,1:T(2,128)}, u32[]{:S(2)}) copy-start(f32[3,2]{0,1:T(2,128)} %param.33) | copy-start | bytes 76
  28.3 16.9 %copy-start.24 = (s32[3]{0:T(128)S(1)}, s32[3]{0:T(128)}, u32[]{:S(2)}) copy-start(s32[3]{0:T(128)} %param.20) | copy-start | bytes 40
  29.0 22.6 %copy-start.11 = (f32[2,512]{1,0:T(2,128)}, f32[2,512]{1,0:T(2,128)S(1)}, u32[]{:S(2)}) copy-start(f32[2,512]{1,0:T(2,128)S(1)} %convert_element_type.247) | copy-start | bytes 12292
  31.1 21.1 %copy-start.17 = (f32[512]{0:T(512)S(1)}, f32[512]{0:T(512)}, u32[]{:S(2)}) copy-start(f32[512]{0:T(512)} %param.27) | copy-start | bytes 6148
  36.8 14.3 %all-to-all-start = ((bf16[16,2,1024]{2,1,0:T(2,128)(2,1)}), bf16[16,2,1024]{2,1,0:T(2,128)(2,1)S(1)}, u32[]{:S(2)}, u32[]{:S(2)}) async-start(bf16[16,2,1024]{2,1,0:T(2,128)(2,1)} %reshape.630), calls=%async_computation | async-start | bytes 131072 | tf_op jit(solution)/shard_map/all_to_all | solution.py:204
  54.1 0.8 copy-start.2
  78.2 5.1 %copy-start.12 = (f32[3]{0:T(128)S(1)}, f32[3]{0:T(128)}, u32[]{:S(2)}) copy-start(f32[3]{0:T(128)} %get-tuple-element.66) | copy-start | bytes 40
  78.2 5.8 %copy-start.14 = (f32[3]{0:T(128)S(1)}, f32[3]{0:T(128)}, u32[]{:S(2)}) copy-start(f32[3]{0:T(128)} %get-tuple-element.67) | copy-start | bytes 40
  81.3 6.8 %collective-permute-start = (bf16[1,2,1024]{2,1,0:T(2,128)(2,1)S(1)}, bf16[1,2,1024]{2,1,0:T(2,128)(2,1)S(1)}, u32[]{:S(2)}, u32[]{:S(2)}) collective-permute-start(bf16[1,2,1024]{2,1,0:T(2,128)(2,1)S(1)} %get-tuple-element.56), channel_id=1, source_target_pairs={{0,1},{1,0},{2,3},{3,2},{4,5},{5,4},{6,7},{7,6},{8,9},{9,8},{10,11... | collective-permute-start | bytes 12296 | tf_op jit(solution)/shard_map/ppermute | solution.py:231
  83.2 34.3 %copy-start.6 = (f32[96,512]{1,0:T(8,128)}, f32[96,512]{1,0:T(8,128)S(1)}, u32[]{:S(2)}) copy-start(f32[96,512]{1,0:T(8,128)S(1)} %add.408) | copy-start | bytes 589828
  84.6 3.8 %collective-permute-start.1 = (bf16[1,2,1024]{2,1,0:T(2,128)(2,1)S(1)}, bf16[1,2,1024]{2,1,0:T(2,128)(2,1)S(1)}, u32[]{:S(2)}, u32[]{:S(2)}) collective-permute-start(bf16[1,2,1024]{2,1,0:T(2,128)(2,1)S(1)} %get-tuple-element.55), channel_id=1, source_target_pairs={{0,2},{1,3},{2,0},{3,1},{4,6},{5,7},{6,4},{7,5},{8,10},{9,11},{10,... | collective-permute-start | bytes 12296 | tf_op jit(solution)/shard_map/ppermute | solution.py:231
  84.7 6.1 %collective-permute-start.2 = (bf16[1,2,1024]{2,1,0:T(2,128)(2,1)S(1)}, bf16[1,2,1024]{2,1,0:T(2,128)(2,1)S(1)}, u32[]{:S(2)}, u32[]{:S(2)}) collective-permute-start(bf16[1,2,1024]{2,1,0:T(2,128)(2,1)S(1)} %get-tuple-element.54), channel_id=1, source_target_pairs={{0,3},{1,2},{2,1},{3,0},{4,7},{5,6},{6,5},{7,4},{8,11},{9,10},{10,... | collective-permute-start | bytes 12296 | tf_op jit(solution)/shard_map/ppermute | solution.py:231
  86.3 4.8 %collective-permute-start.3 = (bf16[1,2,1024]{2,1,0:T(2,128)(2,1)S(1)}, bf16[1,2,1024]{2,1,0:T(2,128)(2,1)S(1)}, u32[]{:S(2)}, u32[]{:S(2)}) collective-permute-start(bf16[1,2,1024]{2,1,0:T(2,128)(2,1)S(1)} %get-tuple-element.53), channel_id=1, source_target_pairs={{0,4},{1,5},{2,6},{3,7},{4,0},{5,1},{6,2},{7,3},{8,12},{9,13},{10,... | collective-permute-start | bytes 12296 | tf_op jit(solution)/shard_map/ppermute | solution.py:231
  86.4 7.2 %collective-permute-start.4 = (bf16[1,2,1024]{2,1,0:T(2,128)(2,1)S(1)}, bf16[1,2,1024]{2,1,0:T(2,128)(2,1)S(1)}, u32[]{:S(2)}, u32[]{:S(2)}) collective-permute-start(bf16[1,2,1024]{2,1,0:T(2,128)(2,1)S(1)} %get-tuple-element.52), channel_id=1, source_target_pairs={{0,5},{1,4},{2,7},{3,6},{4,1},{5,0},{6,3},{7,2},{8,13},{9,12},{10,... | collective-permute-start | bytes 12296 | tf_op jit(solution)/shard_map/ppermute | solution.py:231
  88.1 6.0 %collective-permute-start.5 = (bf16[1,2,1024]{2,1,0:T(2,128)(2,1)S(1)}, bf16[1,2,1024]{2,1,0:T(2,128)(2,1)S(1)}, u32[]{:S(2)}, u32[]{:S(2)}) collective-permute-start(bf16[1,2,1024]{2,1,0:T(2,128)(2,1)S(1)} %get-tuple-element.51), channel_id=1, source_target_pairs={{0,6},{1,7},{2,4},{3,5},{4,2},{5,3},{6,0},{7,1},{8,14},{9,15},{10,... | collective-permute-start | bytes 12296 | tf_op jit(solution)/shard_map/ppermute | solution.py:231
  88.3 9.0 %collective-permute-start.6 = (bf16[1,2,1024]{2,1,0:T(2,128)(2,1)S(1)}, bf16[1,2,1024]{2,1,0:T(2,128)(2,1)S(1)}, u32[]{:S(2)}, u32[]{:S(2)}) collective-permute-start(bf16[1,2,1024]{2,1,0:T(2,128)(2,1)S(1)} %get-tuple-element.50), channel_id=1, source_target_pairs={{0,7},{1,6},{2,5},{3,4},{4,3},{5,2},{6,1},{7,0},{8,15},{9,14},{10,... | collective-permute-start | bytes 12296 | tf_op jit(solution)/shard_map/ppermute | solution.py:231
  90.8 7.2 %collective-permute-start.7 = (bf16[1,2,1024]{2,1,0:T(2,128)(2,1)S(1)}, bf16[1,2,1024]{2,1,0:T(2,128)(2,1)S(1)}, u32[]{:S(2)}, u32[]{:S(2)}) collective-permute-start(bf16[1,2,1024]{2,1,0:T(2,128)(2,1)S(1)} %get-tuple-element.49), channel_id=1, source_target_pairs={{0,8},{1,9},{2,10},{3,11},{4,12},{5,13},{6,14},{7,15},{8,0},{9,1},... | collective-permute-start | bytes 12296 | tf_op jit(solution)/shard_map/ppermute | solution.py:231
  91.1 10.0 %collective-permute-start.8 = (bf16[1,2,1024]{2,1,0:T(2,128)(2,1)S(1)}, bf16[1,2,1024]{2,1,0:T(2,128)(2,1)S(1)}, u32[]{:S(2)}, u32[]{:S(2)}) collective-permute-start(bf16[1,2,1024]{2,1,0:T(2,128)(2,1)S(1)} %get-tuple-element.48), channel_id=1, source_target_pairs={{0,9},{1,8},{2,11},{3,10},{4,13},{5,12},{6,15},{7,14},{8,1},{9,0},... | collective-permute-start | bytes 12296 | tf_op jit(solution)/shard_map/ppermute | solution.py:231
  93.7 8.2 %collective-permute-start.9 = (bf16[1,2,1024]{2,1,0:T(2,128)(2,1)S(1)}, bf16[1,2,1024]{2,1,0:T(2,128)(2,1)S(1)}, u32[]{:S(2)}, u32[]{:S(2)}) collective-permute-start(bf16[1,2,1024]{2,1,0:T(2,128)(2,1)S(1)} %get-tuple-element.47), channel_id=1, source_target_pairs={{0,10},{1,11},{2,8},{3,9},{4,14},{5,15},{6,12},{7,13},{8,2},{9,3},... | collective-permute-start | bytes 12296 | tf_op jit(solution)/shard_map/ppermute | solution.py:231
  94.1 11.6 %collective-permute-start.10 = (bf16[1,2,1024]{2,1,0:T(2,128)(2,1)S(1)}, bf16[1,2,1024]{2,1,0:T(2,128)(2,1)S(1)}, u32[]{:S(2)}, u32[]{:S(2)}) collective-permute-start(bf16[1,2,1024]{2,1,0:T(2,128)(2,1)S(1)} %get-tuple-element.46), channel_id=1, source_target_pairs={{0,11},{1,10},{2,9},{3,8},{4,15},{5,14},{6,13},{7,12},{8,3},{9,2},... | collective-permute-start | bytes 12296 | tf_op jit(solution)/shard_map/ppermute | solution.py:231
  97.3 8.4 %collective-permute-start.11 = (bf16[1,2,1024]{2,1,0:T(2,128)(2,1)S(1)}, bf16[1,2,1024]{2,1,0:T(2,128)(2,1)S(1)}, u32[]{:S(2)}, u32[]{:S(2)}) collective-permute-start(bf16[1,2,1024]{2,1,0:T(2,128)(2,1)S(1)} %get-tuple-element.45), channel_id=1, source_target_pairs={{0,12},{1,13},{2,14},{3,15},{4,8},{5,9},{6,10},{7,11},{8,4},{9,5},... | collective-permute-start | bytes 12296 | tf_op jit(solution)/shard_map/ppermute | solution.py:231
  98.0 7.8 %collective-permute-start.12 = (bf16[1,2,1024]{2,1,0:T(2,128)(2,1)S(1)}, bf16[1,2,1024]{2,1,0:T(2,128)(2,1)S(1)}, u32[]{:S(2)}, u32[]{:S(2)}) collective-permute-start(bf16[1,2,1024]{2,1,0:T(2,128)(2,1)S(1)} %get-tuple-element.44), channel_id=1, source_target_pairs={{0,13},{1,12},{2,15},{3,14},{4,9},{5,8},{6,11},{7,10},{8,5},{9,4},... | collective-permute-start | bytes 12296 | tf_op jit(solution)/shard_map/ppermute | solution.py:231
  101.1 6.4 %collective-permute-start.13 = (bf16[1,2,1024]{2,1,0:T(2,128)(2,1)S(1)}, bf16[1,2,1024]{2,1,0:T(2,128)(2,1)S(1)}, u32[]{:S(2)}, u32[]{:S(2)}) collective-permute-start(bf16[1,2,1024]{2,1,0:T(2,128)(2,1)S(1)} %get-tuple-element.43), channel_id=1, source_target_pairs={{0,14},{1,15},{2,12},{3,13},{4,10},{5,11},{6,8},{7,9},{8,6},{9,7},... | collective-permute-start | bytes 12296 | tf_op jit(solution)/shard_map/ppermute | solution.py:231
  101.8 5.8 %collective-permute-start.14 = (bf16[1,2,1024]{2,1,0:T(2,128)(2,1)S(1)}, bf16[1,2,1024]{2,1,0:T(2,128)(2,1)S(1)}, u32[]{:S(2)}, u32[]{:S(2)}) collective-permute-start(bf16[1,2,1024]{2,1,0:T(2,128)(2,1)S(1)} %get-tuple-element.42), channel_id=1, source_target_pairs={{0,15},{1,14},{2,13},{3,12},{4,11},{5,10},{6,9},{7,8},{8,7},{9,6},... | collective-permute-start | bytes 12296 | tf_op jit(solution)/shard_map/ppermute | solution.py:231
  119.5 2.6 %copy-start.8 = (bf16[1,32,1500]{2,1,0:T(8,128)(2,1)}, bf16[1,32,1500]{2,1,0:T(8,128)(2,1)S(1)}, u32[]{:S(2)}) copy-start(bf16[1,32,1500]{2,1,0:T(8,128)(2,1)S(1)} %add_convert_fusion.1) | copy-start | bytes 288004
  124.1 4.3 %copy-start.3 = (bf16[512,512]{1,0:T(8,128)(2,1)S(1)}, bf16[512,512]{1,0:T(8,128)(2,1)}, u32[]{:S(2)}) copy-start(bf16[512,512]{1,0:T(8,128)(2,1)} %param.26) | copy-start | bytes 1572868
  126.5 17.4 %copy-start.18 = (f32[512]{0:T(512)S(1)}, f32[512]{0:T(512)}, u32[]{:S(2)}) copy-start(f32[512]{0:T(512)} %param.27) | copy-start | bytes 6148
  146.8 4.7 %copy-start.10 = (f32[64,64]{0,1:T(8,128)S(1)}, f32[64,64]{0,1:T(8,128)}, u32[]{:S(2)}) copy-start(f32[64,64]{0,1:T(8,128)} %compare_convert_fusion) | copy-start | bytes 49156
  147.8 5.4 %copy-start.4 = (bf16[512,512]{1,0:T(8,128)(2,1)S(1)}, bf16[512,512]{1,0:T(8,128)(2,1)}, u32[]{:S(2)}) copy-start(bf16[512,512]{1,0:T(8,128)(2,1)} %param.29) | copy-start | bytes 1572868
  149.4 4.3 %copy-start.19 = (f32[512]{0:T(512)S(1)}, f32[512]{0:T(512)}, u32[]{:S(2)}) copy-start(f32[512]{0:T(512)} %param.30) | copy-start | bytes 6148
  153.7 26.8 %copy-start.13 = (f32[3]{0:T(128)S(1)}, f32[3]{0:T(128)}, u32[]{:S(2)}) copy-start(f32[3]{0:T(128)} %get-tuple-element.66) | copy-start | bytes 40
  153.7 26.8 %copy-start.15 = (f32[3]{0:T(128)S(1)}, f32[3]{0:T(128)}, u32[]{:S(2)}) copy-start(f32[3]{0:T(128)} %get-tuple-element.67) | copy-start | bytes 40
  156.3 26.1 %copy-start.5 = (bf16[512,500]{0,1:T(8,128)(2,1)S(1)}, bf16[512,500]{0,1:T(8,128)(2,1)}, u32[]{:S(2)}) copy-start(bf16[512,500]{0,1:T(8,128)(2,1)} %param.35) | copy-start | bytes 1536004
  156.3 26.1 %copy-start.7 = (f32[96,512]{1,0:T(8,128)S(1)}, f32[96,512]{1,0:T(8,128)}, u32[]{:S(2)}) copy-start(f32[96,512]{1,0:T(8,128)} %copy-done.6) | copy-start | bytes 589828
  156.3 26.1 %copy-start.20 = (f32[512]{0:T(512)S(1)}, f32[512]{0:T(512)}, u32[]{:S(2)}) copy-start(f32[512]{0:T(512)} %param.34) | copy-start | bytes 6148
  156.3 26.1 %copy-start.21 = (f32[96]{0:T(128)S(1)}, f32[96]{0:T(128)}, u32[]{:S(2)}) copy-start(f32[96]{0:T(128)} %mul.526) | copy-start | bytes 1156
  156.3 26.0 %copy-start.22 = (f32[96]{0:T(128)S(1)}, f32[96]{0:T(128)}, u32[]{:S(2)}) copy-start(f32[96]{0:T(128)} %mul.600) | copy-start | bytes 1156
  156.8 3.6 %collective-permute-start.15 = (bf16[1,2,1024]{2,1,0:T(2,128)(2,1)S(1)}, bf16[1,2,1024]{2,1,0:T(2,128)(2,1)S(1)}, u32[]{:S(2)}, u32[]{:S(2)}) collective-permute-start(bf16[1,2,1024]{2,1,0:T(2,128)(2,1)S(1)} %get-tuple-element.30), channel_id=1, source_target_pairs={{0,1},{1,0},{2,3},{3,2},{4,5},{5,4},{6,7},{7,6},{8,9},{9,8},{10,11... | collective-permute-start | bytes 12296 | tf_op jit(solution)/shard_map/ppermute | solution.py:231
  156.9 3.8 %collective-permute-start.16 = (bf16[1,2,1024]{2,1,0:T(2,128)(2,1)S(1)}, bf16[1,2,1024]{2,1,0:T(2,128)(2,1)S(1)}, u32[]{:S(2)}, u32[]{:S(2)}) collective-permute-start(bf16[1,2,1024]{2,1,0:T(2,128)(2,1)S(1)} %get-tuple-element.29), channel_id=1, source_target_pairs={{0,2},{1,3},{2,0},{3,1},{4,6},{5,7},{6,4},{7,5},{8,10},{9,11},{10,... | collective-permute-start | bytes 12296 | tf_op jit(solution)/shard_map/ppermute | solution.py:231
  157.1 6.1 %collective-permute-start.17 = (bf16[1,2,1024]{2,1,0:T(2,128)(2,1)S(1)}, bf16[1,2,1024]{2,1,0:T(2,128)(2,1)S(1)}, u32[]{:S(2)}, u32[]{:S(2)}) collective-permute-start(bf16[1,2,1024]{2,1,0:T(2,128)(2,1)S(1)} %get-tuple-element.28), channel_id=1, source_target_pairs={{0,3},{1,2},{2,1},{3,0},{4,7},{5,6},{6,5},{7,4},{8,11},{9,10},{10,... | collective-permute-start | bytes 12296 | tf_op jit(solution)/shard_map/ppermute | solution.py:231
  158.8 4.8 %collective-permute-start.18 = (bf16[1,2,1024]{2,1,0:T(2,128)(2,1)S(1)}, bf16[1,2,1024]{2,1,0:T(2,128)(2,1)S(1)}, u32[]{:S(2)}, u32[]{:S(2)}) collective-permute-start(bf16[1,2,1024]{2,1,0:T(2,128)(2,1)S(1)} %get-tuple-element.27), channel_id=1, source_target_pairs={{0,4},{1,5},{2,6},{3,7},{4,0},{5,1},{6,2},{7,3},{8,12},{9,13},{10,... | collective-permute-start | bytes 12296 | tf_op jit(solution)/shard_map/ppermute | solution.py:231
  158.9 7.1 %collective-permute-start.19 = (bf16[1,2,1024]{2,1,0:T(2,128)(2,1)S(1)}, bf16[1,2,1024]{2,1,0:T(2,128)(2,1)S(1)}, u32[]{:S(2)}, u32[]{:S(2)}) collective-permute-start(bf16[1,2,1024]{2,1,0:T(2,128)(2,1)S(1)} %get-tuple-element.26), channel_id=1, source_target_pairs={{0,5},{1,4},{2,7},{3,6},{4,1},{5,0},{6,3},{7,2},{8,13},{9,12},{10,... | collective-permute-start | bytes 12296 | tf_op jit(solution)/shard_map/ppermute | solution.py:231
  160.5 6.0 %collective-permute-start.20 = (bf16[1,2,1024]{2,1,0:T(2,128)(2,1)S(1)}, bf16[1,2,1024]{2,1,0:T(2,128)(2,1)S(1)}, u32[]{:S(2)}, u32[]{:S(2)}) collective-permute-start(bf16[1,2,1024]{2,1,0:T(2,128)(2,1)S(1)} %get-tuple-element.25), channel_id=1, source_target_pairs={{0,6},{1,7},{2,4},{3,5},{4,2},{5,3},{6,0},{7,1},{8,14},{9,15},{10,... | collective-permute-start | bytes 12296 | tf_op jit(solution)/shard_map/ppermute | solution.py:231
  160.7 9.1 %collective-permute-start.21 = (bf16[1,2,1024]{2,1,0:T(2,128)(2,1)S(1)}, bf16[1,2,1024]{2,1,0:T(2,128)(2,1)S(1)}, u32[]{:S(2)}, u32[]{:S(2)}) collective-permute-start(bf16[1,2,1024]{2,1,0:T(2,128)(2,1)S(1)} %get-tuple-element.24), channel_id=1, source_target_pairs={{0,7},{1,6},{2,5},{3,4},{4,3},{5,2},{6,1},{7,0},{8,15},{9,14},{10,... | collective-permute-start | bytes 12296 | tf_op jit(solution)/shard_map/ppermute | solution.py:231
  163.3 7.1 %collective-permute-start.22 = (bf16[1,2,1024]{2,1,0:T(2,128)(2,1)S(1)}, bf16[1,2,1024]{2,1,0:T(2,128)(2,1)S(1)}, u32[]{:S(2)}, u32[]{:S(2)}) collective-permute-start(bf16[1,2,1024]{2,1,0:T(2,128)(2,1)S(1)} %get-tuple-element.23), channel_id=1, source_target_pairs={{0,8},{1,9},{2,10},{3,11},{4,12},{5,13},{6,14},{7,15},{8,0},{9,1},... | collective-permute-start | bytes 12296 | tf_op jit(solution)/shard_map/ppermute | solution.py:231
  163.6 9.9 %collective-permute-start.23 = (bf16[1,2,1024]{2,1,0:T(2,128)(2,1)S(1)}, bf16[1,2,1024]{2,1,0:T(2,128)(2,1)S(1)}, u32[]{:S(2)}, u32[]{:S(2)}) collective-permute-start(bf16[1,2,1024]{2,1,0:T(2,128)(2,1)S(1)} %get-tuple-element.22), channel_id=1, source_target_pairs={{0,9},{1,8},{2,11},{3,10},{4,13},{5,12},{6,15},{7,14},{8,1},{9,0},... | collective-permute-start | bytes 12296 | tf_op jit(solution)/shard_map/ppermute | solution.py:231
  166.0 8.2 %collective-permute-start.24 = (bf16[1,2,1024]{2,1,0:T(2,128)(2,1)S(1)}, bf16[1,2,1024]{2,1,0:T(2,128)(2,1)S(1)}, u32[]{:S(2)}, u32[]{:S(2)}) collective-permute-start(bf16[1,2,1024]{2,1,0:T(2,128)(2,1)S(1)} %get-tuple-element.21), channel_id=1, source_target_pairs={{0,10},{1,11},{2,8},{3,9},{4,14},{5,15},{6,12},{7,13},{8,2},{9,3},... | collective-permute-start | bytes 12296 | tf_op jit(solution)/shard_map/ppermute | solution.py:231
  166.5 11.7 %collective-permute-start.25 = (bf16[1,2,1024]{2,1,0:T(2,128)(2,1)S(1)}, bf16[1,2,1024]{2,1,0:T(2,128)(2,1)S(1)}, u32[]{:S(2)}, u32[]{:S(2)}) collective-permute-start(bf16[1,2,1024]{2,1,0:T(2,128)(2,1)S(1)} %get-tuple-element.20), channel_id=1, source_target_pairs={{0,11},{1,10},{2,9},{3,8},{4,15},{5,14},{6,13},{7,12},{8,3},{9,2},... | collective-permute-start | bytes 12296 | tf_op jit(solution)/shard_map/ppermute | solution.py:231
  169.8 8.4 %collective-permute-start.26 = (bf16[1,2,1024]{2,1,0:T(2,128)(2,1)S(1)}, bf16[1,2,1024]{2,1,0:T(2,128)(2,1)S(1)}, u32[]{:S(2)}, u32[]{:S(2)}) collective-permute-start(bf16[1,2,1024]{2,1,0:T(2,128)(2,1)S(1)} %get-tuple-element.19), channel_id=1, source_target_pairs={{0,12},{1,13},{2,14},{3,15},{4,8},{5,9},{6,10},{7,11},{8,4},{9,5},... | collective-permute-start | bytes 12296 | tf_op jit(solution)/shard_map/ppermute | solution.py:231
  170.4 7.8 %collective-permute-start.27 = (bf16[1,2,1024]{2,1,0:T(2,128)(2,1)S(1)}, bf16[1,2,1024]{2,1,0:T(2,128)(2,1)S(1)}, u32[]{:S(2)}, u32[]{:S(2)}) collective-permute-start(bf16[1,2,1024]{2,1,0:T(2,128)(2,1)S(1)} %get-tuple-element.18), channel_id=1, source_target_pairs={{0,13},{1,12},{2,15},{3,14},{4,9},{5,8},{6,11},{7,10},{8,5},{9,4},... | collective-permute-start | bytes 12296 | tf_op jit(solution)/shard_map/ppermute | solution.py:231
  173.5 6.4 %collective-permute-start.28 = (bf16[1,2,1024]{2,1,0:T(2,128)(2,1)S(1)}, bf16[1,2,1024]{2,1,0:T(2,128)(2,1)S(1)}, u32[]{:S(2)}, u32[]{:S(2)}) collective-permute-start(bf16[1,2,1024]{2,1,0:T(2,128)(2,1)S(1)} %get-tuple-element.17), channel_id=1, source_target_pairs={{0,14},{1,15},{2,12},{3,13},{4,10},{5,11},{6,8},{7,9},{8,6},{9,7},... | collective-permute-start | bytes 12296 | tf_op jit(solution)/shard_map/ppermute | solution.py:231
  174.3 5.8 %collective-permute-start.29 = (bf16[1,2,1024]{2,1,0:T(2,128)(2,1)S(1)}, bf16[1,2,1024]{2,1,0:T(2,128)(2,1)S(1)}, u32[]{:S(2)}, u32[]{:S(2)}) collective-permute-start(bf16[1,2,1024]{2,1,0:T(2,128)(2,1)S(1)} %get-tuple-element.16), channel_id=1, source_target_pairs={{0,15},{1,14},{2,13},{3,12},{4,11},{5,10},{6,9},{7,8},{8,7},{9,6},... | collective-permute-start | bytes 12296 | tf_op jit(solution)/shard_map/ppermute | solution.py:231
  180.4 3.3 %copy-start.9 = (bf16[1,32,1500]{2,1,0:T(8,128)(2,1)S(1)}, bf16[1,32,1500]{2,1,0:T(8,128)(2,1)}, u32[]{:S(2)}) copy-start(bf16[1,32,1500]{2,1,0:T(8,128)(2,1)} %copy-done.8) | copy-start | bytes 288004
